TPU v7x, 256 devices: a whole 4x4x8 slice. The times are simulated.
256 devices in a mesh: ctx: 32 (over x, y, z_lo), tp: 8 (over z_hi, core).
Axes of the slice: x: 4, y: 4, z: 8 (z_hi: 4, z_lo: 2; z = z_hi * 2 + z_lo), core: 2. Of those that a mesh axis runs over, the one named last changes fastest.
Arguments:
- features: bfloat16 [8192, 8192], P('ctx', 'tp'), may hold values from -6 to 6
- inner: bfloat16 [8192, 8192], P('ctx', 'tp'), may hold values from -6 to 6
- w_bc: bfloat16 [8192, 2, 1024], P('ctx', None, 'tp'), may hold values from -0.005859375 to 0.005859375
- w_dt: bfloat16 [8192, 128], P('ctx', 'tp'), may hold values from -0.0625 to 0.0625
- dt_bias: float32 [128], P('tp'), may hold values from -4 to 0
- decay_rate: float32 [128], P('tp'), may hold values from 0.00012207031 to 1
- skip: float32 [128], P('tp'), may hold values from 0.5 to 1.5
- cotangent: bfloat16 [8192, 8192], P('ctx', 'tp'), may hold values from -6 to 6
- fisher: float32 [8192, 2, 1024], P('ctx', None, 'tp'), may hold values from 0.5 to 4
- importance: float32 [8192, 2, 1024], P('ctx', None, 'tp'), may hold values from 0 to 10
Outputs:
- outputs: bfloat16 [8192, 8192], P('ctx', 'tp')
- grad_inner: bfloat16 [8192, 8192], P('ctx', 'tp')
- grad_features: bfloat16 [8192, 8192], P('ctx', 'tp')
- weight_new: float32 [8192, 2, 1024], P('ctx', None, 'tp')
- fisher_new: float32 [8192, 2, 1024], P('ctx', None, 'tp')
- importance_new: float32 [8192, 2, 1024], P('ctx', None, 'tp')
All inputs are finite; a program needn't handle non-finite values.
Results may differ from a plain program's by a relative error of at most 0.014.
Values may be sent and summed in bfloat16 or wider, within the bound.
A program may use at most 128 MiB of HBM per device.

v0:
```python
from functools import partial
import math

import jax
import jax.numpy as jnp
from jax import lax
from jax.sharding import Mesh
from jax.sharding import PartitionSpec as P

HEADS = 128
P_SIZE = 64
N = 128
G = 8
SPAN = 256
CTX = ("ctx_0", "ctx_1", "ctx_2")


HIGH = lax.Precision.HIGHEST
MIX = 0.25
STEP = 0.1
EPS = 1e-06


def in_one_piece(arrays, axis, dim, along):
    widths = [math.prod(a.shape[along:]) for a in arrays]
    both = jnp.concatenate(
        [a.reshape(*a.shape[:along], w) for a, w in zip(arrays, widths)], axis=along
    )
    whole = lax.all_gather(both, axis, axis=dim, tiled=True)
    blocks = jnp.split(whole, [sum(widths[:k]) for k in range(1, len(widths))], axis=along)
    return tuple(
        (b.reshape(*whole.shape[:along], *a.shape[along:]) for a, b in zip(arrays, blocks))
    )


def nothing_yet(x, identity):
    return jax.tree.map(
        lambda part, zero: jnp.zeros_like(part) + jnp.asarray(zero, part.dtype), x, identity
    )


def prefix_by_axis(x, axes, combine, identity, reverse):
    before = start = nothing_yet(x, identity)
    running = x
    for axis in reversed(axes):
        size, mine = (lax.axis_size(axis), lax.axis_index(axis))
        pieces = jax.tree.map(lambda part: lax.all_gather(part, axis), running)
        inside, running = (start, start)
        for k in reversed(range(size)) if reverse else range(size):
            passed = k > mine if reverse else k < mine
            running = combine(running, jax.tree.map(lambda part: part[k], pieces))
            inside = jax.tree.map(lambda new, old: jnp.where(passed, new, old), running, inside)
        before = combine(inside, before)
    return before


def in_order(blocks, dim):
    shape = list(blocks.shape[1:])
    shape[dim] *= blocks.shape[0]
    return jnp.moveaxis(blocks, 0, dim).reshape(shape)


def gather_together(arrays, axis, dims):
    ravelled = jnp.concatenate([a.reshape(-1) for a in arrays])
    lines, at, gathered = (lax.all_gather(ravelled, axis), 0, [])
    for a, dim in zip(arrays, dims):
        blocks = lines[:, at : at + a.size].reshape(-1, *a.shape)
        gathered.append(in_order(blocks, dim))
        at += a.size
    return tuple(gathered)


def summed_rows(x, axes, dim):
    for axis in axes:
        x = lax.psum_scatter(x, axis, scatter_dimension=dim, tiled=True)
    return x


def span_pass(dt_bias, rate, state, blocks):
    xc, bc, cc, zc = blocks
    dt = jax.nn.softplus(zc + dt_bias)
    logs = -rate * dt
    cums = jnp.cumsum(logs, axis=0)
    length = xc.shape[0]
    rows = lax.broadcasted_iota(jnp.int32, (length, length), 0)
    cols = lax.broadcasted_iota(jnp.int32, (length, length), 1)
    causal = rows >= cols
    scores = jnp.einsum("ign,jgn->gij", cc, bc, precision=HIGH)
    order = jnp.transpose(cums, (1, 2, 0))
    diff = order[:, :, :, None] - order[:, :, None, :]
    decays = jnp.where(causal, jnp.exp(jnp.where(causal, diff, 0.0)), 0.0)
    weights = decays * scores[:, None] * jnp.transpose(dt, (1, 2, 0))[:, :, None, :]
    intra = jnp.einsum("ghij,jghp->ighp", weights, xc, precision=HIGH)
    inter = jnp.exp(cums)[..., None] * jnp.einsum("ign,ghpn->ighp", cc, state, precision=HIGH)
    last = cums[-1]
    tail = jnp.exp(last[None] - cums) * dt
    fresh = jnp.einsum("jghp,jgh,jgn->ghpn", xc, tail, bc, precision=HIGH)
    new_state = jnp.exp(last)[..., None, None] * state + fresh
    return (new_state, intra + inter)


def run_spans(x, b, c, z, dt_bias, rate):
    tokens, groups, heads, width = x.shape
    count = tokens // SPAN
    state0 = jnp.zeros((groups, heads, width, b.shape[-1]), jnp.float32)
    blocks = (
        x.reshape(count, SPAN, groups, heads, width),
        b.reshape(count, SPAN, groups, b.shape[-1]),
        c.reshape(count, SPAN, groups, c.shape[-1]),
        z.reshape(count, SPAN, groups, heads),
    )
    final, ys = lax.scan(partial(span_pass, dt_bias, rate), state0, blocks)
    return (ys.reshape(tokens, groups, heads, width), final)


def link(earlier, later):
    return (earlier[0] * later[0], later[0][..., None, None] * earlier[1] + later[1])


def contract_last(left, right):
    return lax.dot_general(
        left, right, (((1,), (1,)), ((), ())), preferred_element_type=jnp.float32
    )


def rwalk(weight, grad, fisher, importance):
    fisher_new = MIX * grad * grad + (1.0 - MIX) * fisher
    delta = -STEP * grad
    importance_new = importance + -grad * delta / (0.5 * fisher_new * delta * delta + EPS)
    weight_new = weight.astype(jnp.float32) + delta
    return (weight_new, fisher_new, importance_new)


def local(features, inner, w_bc, w_dt, dt_bias, decay_rate, skip, cotangent, fisher, importance):
    tokens = features.shape[0]
    groups = w_bc.shape[2] // N
    per_group = HEADS // G
    whole = lax.all_gather(features, "tp", axis=1, tiled=True)
    rows_bc, rows_dt = in_one_piece((w_bc, w_dt), CTX, 0, 1)
    depth = rows_bc.shape[0]
    wide = rows_bc.reshape(depth, 2 * groups * N)
    block_bc, block_dt = (
        lax.all_to_all(wide, "tp", split_axis=0, concat_axis=1, tiled=True),
        lax.all_to_all(rows_dt, "tp", split_axis=0, concat_axis=1, tiled=True),
    )
    proj = jnp.dot(whole, wide, preferred_element_type=jnp.float32)
    proj = lax.optimization_barrier(proj.astype(jnp.bfloat16)).astype(jnp.float32)
    bmat = proj[:, : groups * N].reshape(tokens, groups, N)
    cmat = proj[:, groups * N :].reshape(tokens, groups, N)
    zdt = jnp.dot(whole, rows_dt, preferred_element_type=jnp.float32).reshape(
        tokens, groups, per_group
    )
    bias = dt_bias.reshape(groups, per_group)
    rate = decay_rate.reshape(groups, per_group)
    gain = skip.reshape(groups, per_group)
    xval = inner.astype(jnp.float32).reshape(tokens, groups, per_group, P_SIZE)

    def zero_start(xv, bv, cv, zv):
        core, final = run_spans(xv, bv, cv, zv, bias, rate)
        return (core + gain[..., None] * xv, final)

    def enter(cv, zv, incoming):
        logs = -rate * jax.nn.softplus(zv + bias)
        cums = jnp.cumsum(logs, axis=0)
        added = jnp.exp(cums)[..., None] * jnp.einsum(
            "ign,ghpn->ighp", cv, incoming, precision=HIGH
        )
        return (added, jnp.exp(cums[-1])[..., None, None] * incoming)

    (base, local_state), back_zero = jax.vjp(zero_start, xval, bmat, cmat, zdt)
    decay = jnp.exp(jnp.sum(-rate * jax.nn.softplus(zdt + bias), axis=0))
    identity = (jnp.ones_like(decay), jnp.zeros_like(local_state))
    carried = prefix_by_axis((decay, local_state), CTX, link, identity, False)[1]
    (added, passed), back_enter = jax.vjp(enter, cmat, zdt, carried)
    outputs = (base + added).reshape(tokens, -1).astype(jnp.bfloat16)
    upstream = cotangent.astype(jnp.float32).reshape(xval.shape)
    dc_enter, dz_enter, state_local = back_enter((upstream, jnp.zeros_like(passed)))
    later = prefix_by_axis((decay, state_local), CTX, link, identity, True)[1]
    dz_pass = back_enter((jnp.zeros_like(upstream), later))[1]
    dx, dbm, dc_zero, dz_zero = back_zero((upstream, later))
    dcm = dc_zero + dc_enter
    dz = dz_zero + dz_enter + dz_pass
    grad_inner = dx.reshape(tokens, -1).astype(jnp.bfloat16)
    dproj = jnp.concatenate(
        [dbm.reshape(tokens, groups * N), dcm.reshape(tokens, groups * N)], axis=1
    ).astype(jnp.bfloat16)
    dz_half = dz.reshape(tokens, -1).astype(jnp.bfloat16)
    every_bc, every_dt = gather_together((dproj, dz_half), "tp", (1, 1))
    grad_features = (contract_last(every_bc, block_bc) + contract_last(every_dt, block_dt)).astype(
        jnp.bfloat16
    )
    product = lax.dot_general(
        whole, dproj, (((0,), (0,)), ((), ())), preferred_element_type=jnp.float32
    )
    summed = summed_rows(product, CTX, 0)
    grad = summed.reshape(w_bc.shape) / (tokens * lax.axis_size(CTX))
    weight_new, fisher_new, importance_new = rwalk(w_bc, grad, fisher, importance)
    return (outputs, grad_inner, grad_features, weight_new, fisher_new, importance_new)


def solution(mesh):
    split = Mesh(mesh.devices.reshape(4, 4, 2, mesh.shape["tp"]), ("ctx_0", "ctx_1", "ctx_2", "tp"))
    placed = (
        P(CTX, "tp"),
        P(CTX, "tp"),
        P(CTX, None, "tp"),
        P(CTX, "tp"),
        P("tp"),
        P("tp"),
        P("tp"),
        P(CTX, "tp"),
        P(CTX, None, "tp"),
        P(CTX, None, "tp"),
    )
    return jax.shard_map(
        local,
        mesh=split,
        in_specs=placed,
        out_specs=(
            P(CTX, "tp"),
            P(CTX, "tp"),
            P(CTX, "tp"),
            P(CTX, None, "tp"),
            P(CTX, None, "tp"),
            P(CTX, None, "tp"),
        ),
        check_vma=False,
    )
```

profile of v0, /device:TPU:110, one launch (start us, length us, event | category | flops | bytes accessed | tf_op | source)
XLA Modules:
  0.0 661.1 jit_solution(10560624996359038437)
XLA Ops:
  9.0 1.4 pad_maximum_fusion
  12.3 50.8 %all-gather.17.cloned.1.call-done = bf16[256,8192]{1,0:T(8,128)(2,1)} async-done(((bf16[256,1024]{1,0:T(8,128)(2,1)}), bf16[256,8192]{1,0:T(8,128)(2,1)}) %all-gather.17.cloned.1.call-update) | async-done | bytes 4194320 | tf_op jit(solution)/shard_map/all_gather | solution.py:138
  63.1 161.4 %all-gather.15.cloned.1.call-done = bf16[8192,272]{0,1:T(8,128)(2,1)} async-done(((bf16[256,272]{0,1:T(8,128)(2,1)}), bf16[8192,272]{0,1:T(8,128)(2,1)}) %all-gather.15.cloned.1.call-update) | async-done | bytes 4456464 | tf_op jit(solution)/shard_map/all_gather | solution.py:29
  224.5 3.5 fusion.246
  229.3 4.8 fusion.54
  234.3 1.4 convolution_add_fusion.1
  236.3 1.4 convolution_add_fusion
  240.4 4.9 all-reduce.3
  245.5 9.4 %all-reduce.4 = f32[64]{0:T(128)S(1)} all-reduce(f32[64]{0:T(128)S(1)} %multiply_dynamic-update-slice_fusion), channel_id=6, replica_groups=mesh['ctx_0'=4,'ctx_1'=4,'ctx_2'=2,'tp'=8] {'ctx_1'}, use_global_device_ids=true, to_apply=%add.4 | all-reduce | flops 64 | bytes 512
  255.6 7.4 %all-gather.27.cloned.1.call-done = f32[32,64,128]{2,1,0:T(8,128)} async-done(((f32[16,64,128]{2,1,0:T(8,128)}), f32[32,64,128]{2,1,0:T(8,128)}) %all-gather.27.cloned.1.call-update) | async-done | bytes 1048592 | tf_op jit(solution)/shard_map/all_gather | solution.py:47
  263.0 2.1 bitcast_add_fusion.30
  265.2 26.9 %all-gather.29.cloned.1.call-done = f32[32,64,128]{2,1,0:T(8,128)} async-done(((f32[16,64,128]{2,1,0:T(8,128)}), f32[32,64,128]{2,1,0:T(8,128)}) %all-gather.29.cloned.1.call-update) | async-done | bytes 1048592 | tf_op jit(solution)/shard_map/all_gather | solution.py:47
  292.1 2.1 bitcast_add_fusion.28
  294.9 33.3 %all-gather.19.cloned.1.call-done = f32[4,1,16,64,128]{4,3,2,1,0:T(8,128)} async-done(((f32[1,1,16,64,128]{4,3,2,1,0:T(8,128)}), f32[4,1,16,64,128]{4,3,2,1,0:T(8,128)}) %all-gather.19.cloned.1.call-update) | async-done | bytes 2097168 | tf_op jit(solution)/shard_map/all_gather | solution.py:47
  328.2 35.6 %all-gather.23.cloned.1.call-done = f32[4,1,16,64,128]{4,3,2,1,0:T(8,128)} async-done(((f32[1,1,16,64,128]{4,3,2,1,0:T(8,128)}), f32[4,1,16,64,128]{4,3,2,1,0:T(8,128)}) %all-gather.23.cloned.1.call-update) | async-done | bytes 2097168 | tf_op jit(solution)/shard_map/all_gather | solution.py:47
  363.9 3.6 multiply_add_fusion
  368.4 2.0 copy.179
  370.4 2.1 copy.192
  376.0 6.7 %all_gather.69 = f32[4,1,16]{2,1,0:T(1,128)S(1)} all-gather(f32[1,1,16]{2,1,0:T(1,128)S(1)} %get-tuple-element.452), channel_id=1, replica_groups=mesh['ctx_0'=4,'ctx_1'=4,'ctx_2'=2,'tp'=8] {'ctx_0'}, dimensions={0}, use_global_device_ids=true | all-gather | bytes 320 | tf_op jit(solution)/shard_map/all_gather | solution.py:47
  382.7 9.7 %all_gather.64 = f32[4,1,16]{2,1,0:T(1,128)S(1)} all-gather(f32[1,1,16]{2,1,0:T(1,128)S(1)} %get-tuple-element.453), channel_id=1, replica_groups=mesh['ctx_0'=4,'ctx_1'=4,'ctx_2'=2,'tp'=8] {'ctx_0'}, dimensions={0}, use_global_device_ids=true | all-gather | bytes 320 | tf_op jit(solution)/shard_map/all_gather | solution.py:47
  392.4 1.4 convolution_bitcast_fusion.7
  397.3 2.9 all-gather.21.cloned.1.call-done
  400.2 3.0 add_add_fusion
  404.0 1.8 convolution_bitcast_fusion.6
  405.8 30.2 %all-gather.25.cloned.1.call-done = f32[4,1,16,64,128]{4,3,2,1,0:T(8,128)} async-done(((f32[1,1,16,64,128]{4,3,2,1,0:T(8,128)}), f32[4,1,16,64,128]{4,3,2,1,0:T(8,128)}) %all-gather.25.cloned.1.call-update) | async-done | bytes 2097168 | tf_op jit(solution)/shard_map/all_gather | solution.py:47
  435.9 5.4 multiply_reduce_fusion.2
  441.3 1.5 copy.228
  442.8 2.4 fusion.245
  446.3 5.2 fusion.10
  452.2 4.1 fusion.57
  456.3 4.6 convolution_bitcast_fusion
  462.6 6.5 all-to-all-start.1
  469.1 4.6 split.9
  473.6 6.5 copy.208
  480.8 7.4 %all-to-all-start = ((bf16[8,1024,256]{2,1,0:T(8,128)(2,1)}), bf16[8,1024,256]{2,1,0:T(8,128)(2,1)}, u32[]{:S(2)}, u32[]{:S(2)}) async-start(bf16[8,1024,256]{2,1,0:T(8,128)(2,1)} %bitcast.574), calls=%async_computation | async-start | bytes 8388608 | tf_op jit(solution)/shard_map/all_to_all | solution.py:143
  488.3 55.9 %reduce-scatter.4.cloned.1.call-done = f32[2048,256]{0,1:T(8,128)} async-done(((f32[8192,256]{0,1:T(8,128)}), f32[2048,256]{0,1:T(8,128)}) %reduce-scatter.4.cloned.1.call-update) | async-done | bytes 2097168 | tf_op jit(solution)/shard_map/reduce_scatter | solution.py:75
  544.5 1.6 convolution_bitcast_fusion.2
  546.2 2.2 multiply_reduce_fusion.5
  548.4 1.5 copy.197
  549.8 1.5 copy.202
  551.3 1.5 copy.205
  552.8 1.5 copy.198
  554.2 1.5 copy.199
  555.7 1.5 copy.195
  559.1 5.1 multiply_reduce_fusion.8
  565.6 1.6 copy.200
  567.1 3.8 reduce-window.54
  570.9 1.6 copy.203
  572.5 3.8 reduce-window.56
  576.3 1.5 copy.204
  577.7 1.4 slice_reduce_fusion.1
  580.3 1.5 copy.201
  584.4 1.6 copy.206
  586.0 3.8 reduce-window.58
  589.8 1.5 copy.207
  591.2 1.4 slice_reduce_fusion
  595.9 2.0 fusion.206
  598.8 1.6 pad_maximum_fusion.1
  601.6 5.9 fusion.50
  607.6 4.3 fusion.32
  614.2 15.7 %all-gather.31.cloned.1.call-done = bf16[557056]{0:T(1024)(128)(2,1)} async-done(((bf16[69632]{0:T(1024)(128)(2,1)}), bf16[557056]{0:T(1024)(128)(2,1)}) %all-gather.31.cloned.1.call-update) | async-done | bytes 1114128 | tf_op jit(solution)/shard_map/all_gather | solution.py:65
  629.9 1.7 reshape.2054
  633.6 4.6 fusion.47
  638.3 13.2 %reduce-scatter.8.cloned.1.call-done = f32[256,256]{0,1:T(8,128)} async-done(((f32[512,256]{0,1:T(8,128)}), f32[256,256]{0,1:T(8,128)}) %reduce-scatter.8.cloned.1.call-update) | async-done | bytes 262160 | tf_op jit(solution)/shard_map/reduce_scatter | solution.py:75
  (236 shorter events, 40.7 us)
Async XLA Ops:
  7.2 55.9 %all-gather.17.cloned.1.call-start = ((), (), s32[]{:S(2)}) async-start(), calls=%async_computation.6 | async-start | bytes 4718592 | tf_op jit(solution)/shard_map/all_gather | solution.py:138
  7.9 216.6 %all-gather.15.cloned.1.call-start = ((), (), s32[]{:S(2)}) async-start(), calls=%async_computation.5 | async-start | bytes 4595712 | tf_op jit(solution)/shard_map/all_gather | solution.py:29
  10.4 252.7 %all-gather.27.cloned.1.call-start = ((), (), s32[]{:S(2)}) async-start(), calls=%async_computation.14 | async-start | bytes 1572864 | tf_op jit(solution)/shard_map/all_gather | solution.py:47
  11.1 216.9 %copy-start.65 = (f32[16]{0:T(128)}, f32[16]{0:T(128)S(1)}, u32[]{:S(2)}) copy-start(f32[16]{0:T(128)S(1)} %neg.70) | copy-start | bytes 196
  12.3 222.0 %copy-start.5 = (f32[256,1024]{0,1:T(8,128)}, f32[256,1024]{0,1:T(8,128)S(1)}, u32[]{:S(2)}) copy-start(f32[256,1024]{0,1:T(8,128)S(1)} %copy.184) | copy-start | bytes 3145732
  228.0 6.1 copy-start.15
  228.9 213.9 %copy-start.11 = (f32[16,1,2,128]{0,3,2,1:T(8,128)}, f32[16,1,2,128]{0,3,2,1:T(8,128)S(1)}, u32[]{:S(2)}) copy-start(f32[16,1,2,128]{0,3,2,1:T(8,128)S(1)} %copy.180) | copy-start | bytes 49156
  229.0 7.0 %copy-start.19 = (f32[16,1,256]{0,2,1:T(8,128)}, f32[16,1,256]{0,2,1:T(8,128)S(1)}, u32[]{:S(2)}) copy-start(f32[16,1,256]{0,2,1:T(8,128)S(1)} %bitcast_add_fusion.43) | copy-start | bytes 49156
  229.3 6.5 copy-start.2
  234.1 217.6 %copy-start.13 = (bf16[256,256]{0,1:T(8,128)(2,1)}, bf16[256,256]{0,1:T(8,128)(2,1)S(1)}, u32[]{:S(2)}) copy-start(bf16[256,256]{0,1:T(8,128)(2,1)S(1)} %fusion.54) | copy-start | bytes 393220
  234.3 30.9 %copy-start.42 = (f32[256,16]{0,1:T(8,128)}, f32[256,16]{0,1:T(8,128)S(1)}, u32[]{:S(2)}) copy-start(f32[256,16]{0,1:T(8,128)S(1)} %copy.185) | copy-start | bytes 49156
  235.8 56.3 %all-gather.29.cloned.1.call-start = ((), (), s32[]{:S(2)}) async-start(), calls=%async_computation.15 | async-start | bytes 1572864 | tf_op jit(solution)/shard_map/all_gather | solution.py:47
  237.7 90.5 %all-gather.19.cloned.1.call-start = ((), (), s32[]{:S(2)}) async-start(), calls=%async_computation.7 | async-start | bytes 2621440 | tf_op jit(solution)/shard_map/all_gather | solution.py:47
  254.9 108.9 %copy-start.41 = (f32[64]{0:T(128)}, f32[64]{0:T(128)S(1)}, u32[]{:S(2)}) copy-start(f32[64]{0:T(128)S(1)} %all-reduce.4) | copy-start | bytes 772
  255.6 108.3 %copy-start.49 = (f32[16]{0:T(128)}, f32[16]{0:T(128)S(1)}, u32[]{:S(2)}) copy-start(f32[16]{0:T(128)S(1)} %get-tuple-element.454) | copy-start | bytes 196
  255.6 108.3 %copy-start.50 = (f32[16]{0:T(128)}, f32[16]{0:T(128)S(1)}, u32[]{:S(2)}) copy-start(f32[16]{0:T(128)S(1)} %get-tuple-element.456) | copy-start | bytes 196
  255.6 108.3 %copy-start.54 = (f32[16]{0:T(128)}, f32[16]{0:T(128)S(1)}, u32[]{:S(2)}) copy-start(f32[16]{0:T(128)S(1)} %get-tuple-element.455) | copy-start | bytes 196
  255.6 108.3 %copy-start.56 = (f32[16]{0:T(128)}, f32[16]{0:T(128)S(1)}, u32[]{:S(2)}) copy-start(f32[16]{0:T(128)S(1)} %get-tuple-element.457) | copy-start | bytes 196
  265.2 98.7 %all-gather.23.cloned.1.call-start = ((), (), s32[]{:S(2)}) async-start(), calls=%async_computation.9 | async-start | bytes 2621440 | tf_op jit(solution)/shard_map/all_gather | solution.py:47
  294.3 105.9 %all-gather.21.cloned.1.call-start = ((), (), s32[]{:S(2)}) async-start(), calls=%async_computation.8 | async-start | bytes 2621440 | tf_op jit(solution)/shard_map/all_gather | solution.py:47
  363.9 36.3 %copy-start.1 = (f32[4,1,16,64,128]{4,3,2,1,0:T(8,128)S(1)}, f32[4,1,16,64,128]{4,3,2,1,0:T(8,128)}, u32[]{:S(2)}) copy-start(f32[4,1,16,64,128]{4,3,2,1,0:T(8,128)} %all-gather.19.cloned.1.call-done) | copy-start | bytes 6291460
  367.6 68.4 %all-gather.25.cloned.1.call-start = ((), (), s32[]{:S(2)}) async-start(), calls=%async_computation.10 | async-start | bytes 2621440 | tf_op jit(solution)/shard_map/all_gather | solution.py:47
  368.3 175.9 %reduce-scatter.4.cloned.1.call-start = ((), (), s32[]{:S(2)}) async-start(), calls=%async_computation.11 | async-start | bytes 10485760 | tf_op jit(solution)/shard_map/reduce_scatter | solution.py:75
  446.1 5.6 copy-start.24
  446.1 5.6 copy-start.32
  446.1 6.0 copy-start.6
  446.1 6.0 copy-start.10
  446.1 6.0 copy-start.17
  446.2 5.9 copy-start.18
  446.2 5.9 copy-start.43
  446.2 5.9 copy-start.51
  446.2 5.9 copy-start.52
  446.2 5.9 copy-start.55
  446.2 5.9 copy-start.57
  446.2 5.9 copy-start.58
  446.2 5.9 copy-start.59
  446.2 5.9 copy-start.60
  446.2 5.9 copy-start.61
  446.3 5.9 copy-start.63
  446.3 5.9 copy-start.64
  452.2 8.7 %copy-start.22 = (bf16[256,128]{0,1:T(8,128)(2,1)}, bf16[256,128]{0,1:T(8,128)(2,1)S(1)}, u32[]{:S(2)}) copy-start(bf16[256,128]{0,1:T(8,128)(2,1)S(1)} %fusion.55) | copy-start | bytes 196612
  462.6 17.5 %all-to-all-start.1 = ((bf16[8,1024,16]{1,2,0:T(8,128)(2,1)}), bf16[8,1024,16]{1,2,0:T(8,128)(2,1)S(1)}, u32[]{:S(2)}, u32[]{:S(2)}) async-start(bf16[8,1024,16]{1,2,0:T(8,128)(2,1)} %bitcast.591), calls=%async_computation.1 | async-start | bytes 524288 | tf_op jit(solution)/shard_map/all_to_all | solution.py:144
  480.8 63.7 %copy-start.14 = (bf16[256,256]{0,1:T(8,128)(2,1)S(1)}, bf16[256,256]{0,1:T(8,128)(2,1)}, u32[]{:S(2)}) copy-start(bf16[256,256]{0,1:T(8,128)(2,1)} %copy-done.13) | copy-start | bytes 393220
  480.8 152.8 %all-to-all-start = ((bf16[8,1024,256]{2,1,0:T(8,128)(2,1)}), bf16[8,1024,256]{2,1,0:T(8,128)(2,1)}, u32[]{:S(2)}, u32[]{:S(2)}) async-start(bf16[8,1024,256]{2,1,0:T(8,128)(2,1)} %bitcast.574), calls=%async_computation | async-start | bytes 8388608 | tf_op jit(solution)/shard_map/all_to_all | solution.py:143
  488.3 68.9 %copy-start.23 = (bf16[256,128]{0,1:T(8,128)(2,1)S(1)}, bf16[256,128]{0,1:T(8,128)(2,1)}, u32[]{:S(2)}) copy-start(bf16[256,128]{0,1:T(8,128)(2,1)} %copy-done.22) | copy-start | bytes 196612
  488.3 68.9 %copy-start.34 = (bf16[256,128]{0,1:T(8,128)(2,1)S(1)}, bf16[256,128]{0,1:T(8,128)(2,1)}, u32[]{:S(2)}) copy-start(bf16[256,128]{0,1:T(8,128)(2,1)} %copy-done.33) | copy-start | bytes 196612
  488.3 119.2 %reduce-scatter.6.cloned.1.call-start = ((), (), s32[]{:S(2)}) async-start(), calls=%async_computation.12 | async-start | bytes 2621440 | tf_op jit(solution)/shard_map/reduce_scatter | solution.py:75
  544.2 85.7 %all-gather.31.cloned.1.call-start = ((), (), s32[]{:S(2)}) async-start(), calls=%async_computation.16 | async-start | bytes 1253376 | tf_op jit(solution)/shard_map/all_gather | solution.py:65
  559.1 36.8 %copy-start.12 = (f32[16,1,2,128]{0,3,2,1:T(8,128)S(1)}, f32[16,1,2,128]{0,3,2,1:T(8,128)}, u32[]{:S(2)}) copy-start(f32[16,1,2,128]{0,3,2,1:T(8,128)} %copy-done.11) | copy-start | bytes 49156
  559.1 36.8 %copy-start.16 = (f32[256,16]{1,0:T(8,128)S(1)}, f32[256,16]{1,0:T(8,128)}, u32[]{:S(2)}) copy-start(f32[256,16]{1,0:T(8,128)} %copy-done.15) | copy-start | bytes 49156
  564.2 37.3 %copy-start.7 = (f32[256,1024]{0,1:T(8,128)S(1)}, f32[256,1024]{0,1:T(8,128)}, u32[]{:S(2)}) copy-start(f32[256,1024]{0,1:T(8,128)} %copy-done.5) | copy-start | bytes 3145732
  564.2 37.3 %copy-start.9 = (f32[256,1,16,64]{0,3,2,1:T(8,128)S(1)}, f32[256,1,16,64]{0,3,2,1:T(8,128)}, u32[]{:S(2)}) copy-start(f32[256,1,16,64]{0,3,2,1:T(8,128)} %copy-done.8) | copy-start | bytes 3145732
  564.2 37.3 %copy-start.21 = (f32[256,1,16,64]{0,3,2,1:T(8,128)S(1)}, f32[256,1,16,64]{0,3,2,1:T(8,128)}, u32[]{:S(2)}) copy-start(f32[256,1,16,64]{0,3,2,1:T(8,128)} %get-tuple-element.467) | copy-start | bytes 3145732
  600.4 51.0 %reduce-scatter.8.cloned.1.call-start = ((), (), s32[]{:S(2)}) async-start(), calls=%async_computation.13 | async-start | bytes 786432 | tf_op jit(solution)/shard_map/reduce_scatter | solution.py:75
  601.6 6.0 copy-start.37
  601.6 6.0 copy-start.44
  601.6 6.0 copy-start.45
  601.6 6.0 copy-start.46
  601.6 6.0 copy-start.48
  607.6 5.7 copy-start.3
  612.3 20.0 %copy-start.40 = (bf16[8,1024,16]{1,2,0:T(8,128)(2,1)S(1)}, bf16[8,1024,16]{1,2,0:T(8,128)(2,1)}, u32[]{:S(2)}) copy-start(bf16[8,1024,16]{1,2,0:T(8,128)(2,1)} %copy-done.39) | copy-start | bytes 786436
  633.6 19.3 %copy-start.25 = (bf16[256,2,128]{2,1,0:T(2,128)(2,1)S(1)}, bf16[256,2,128]{2,1,0:T(2,128)(2,1)}, u32[]{:S(2)}) copy-start(bf16[256,2,128]{2,1,0:T(2,128)(2,1)} %param.12) | copy-start | bytes 393220
  633.6 19.3 %copy-start.35 = (f32[256,2,128]{2,1,0:T(2,128)S(1)}, f32[256,2,128]{2,1,0:T(2,128)}, u32[]{:S(2)}) copy-start(f32[256,2,128]{2,1,0:T(2,128)} %param.19) | copy-start | bytes 786436
  633.6 19.3 %copy-start.36 = (f32[256,2,128]{2,1,0:T(2,128)S(1)}, f32[256,2,128]{2,1,0:T(2,128)}, u32[]{:S(2)}) copy-start(f32[256,2,128]{2,1,0:T(2,128)} %param.18) | copy-start | bytes 786436
  (19 other events, 74.7 us)
Sparse Core Ops, SparseCore 0:
  9.8 53.2 all-gather.16
  65.4 159.0 all-gather.14
  235.9 27.0 all-gather.26
  265.2 26.8 all-gather.28
  294.3 33.8 all-gather.18
  330.5 33.3 all-gather.22
  367.7 32.4 all-gather.20
  402.6 33.3 all-gather.24
  461.1 83.1 reduce-scatter.3
  546.6 32.6 reduce-scatter.5
  600.6 29.3 all-gather.30
  632.3 19.1 reduce-scatter.7
where the time goes:
time: 666 us; the launch traced here: 661 us
  waiting for transfers between devices  435 us (65%)
  local copies, waits for them, and re-layouts  58.4 us (9%)
  matrix products  55 us (8%)
  other arithmetic  50.7 us (8%)
  blocking collectives  30.8 us (5%)
  between operations  16.6 us (2%)
  starting transfers between devices  14.9 us (2%)
    all_gather x1, waiting for transfers between devices, in_one_piece(): whole = lax.all_gather(both, axis, axis=dim, tiled=True)  161 us
    all_gather x6, waiting for transfers between devices, prefix_by_axis(): pieces = jax.tree.map(lambda part: lax.all_gather(part, axis), running)  136 us
    reduce_scatter x3, waiting for transfers between devices, summed_rows(): x = lax.psum_scatter(x, axis, scatter_dimension=dim, tiled=True)  69.1 us
    all_gather x1, waiting for transfers between devices, local(): whole = lax.all_gather(features, 'tp', axis=1, tiled=True)  50.8 us
    another operation x23, local copies, waits for them, and re-layouts  17.6 us
    all_gather x2, blocking collectives, prefix_by_axis(): pieces = jax.tree.map(lambda part: lax.all_gather(part, axis), running)  16.4 us
    another operation x9, other arithmetic  15.8 us
    all_gather x1, waiting for transfers between devices, gather_together(): lines, at, gathered = (lax.all_gather(ravelled, axis), 0, [])  15.7 us
  transfers between devices with their start and end apart: 14, of which 11 were waited for; matrix products, arithmetic and copies ran while one was open for 18% of the time, Pallas kernels for 0%

commit v1 on v0

v1 whole, which is shorter than its diff:
```python
from functools import partial

import jax
import jax.numpy as jnp
from jax import lax
from jax.experimental import pallas as pl
from jax.experimental.pallas import tpu as pltpu
from jax.sharding import Mesh
from jax.sharding import PartitionSpec as P

AXES = ("x", "y", "zl", "zh", "core")
CTX = AXES[:3]
TP = AXES[3:]
DEPTH = 8192
TOKENS = 8192
HEADS = 16
WIDTH = 64
N = 128
SPAN = 256
SPANS = 32
MSG = 272
SLICE = 32
MIX = 0.25
STEP = 0.1
EPS = 1e-06
MESH = pl.DeviceIdType.MESH
BF = jnp.bfloat16
F32 = jnp.float32
HIGH = lax.Precision.HIGHEST
VMEM = pl.BlockSpec(memory_space=pltpu.VMEM)
ANY = pl.BlockSpec(memory_space=pl.ANY)


def place():
    return tuple(lax.axis_index(a) for a in AXES)


def at(x, y, zl, zh, core):
    return {"x": x, "y": y, "zl": zl, "zh": zh, "core": core}


def spread_to(x, y, zl, zh, core):
    return at((x - zh + 4) % 4, 2 * (y % 2) + zl, 1 - core, x, y // 2)


def spread_from(x, y, zl, zh, core):
    return at(zh, 2 * core + y // 2, y % 2, (zh - x + 4) % 4, 1 - zl)


def greet(sources):
    barrier = pltpu.get_barrier_semaphore()
    for device in sources:
        pl.semaphore_signal(barrier, inc=1, device_id=device, device_id_type=MESH)
    return lambda: pl.semaphore_wait(barrier, len(sources))


def remote(src, dst, send, recv, device):
    return pltpu.make_async_remote_copy(
        src_ref=src,
        dst_ref=dst,
        send_sem=send,
        recv_sem=recv,
        device_id=device,
        device_id_type=MESH,
    )


def dot(a, b, dims=((1,), (0,)), precision=None):
    return lax.dot_general(a, b, (dims, ((), ())), precision=precision, preferred_element_type=F32)


NT = ((1,), (1,))
TN = ((0,), (0,))


def wide(rows):
    cols = rows.T
    return jnp.concatenate(
        [jnp.broadcast_to(cols[:, h : h + 1], (SPAN, WIDTH)) for h in range(HEADS)], axis=1
    )


def by_head():
    row = lax.broadcasted_iota(jnp.int32, (HEADS, HEADS * WIDTH), 0)
    col = lax.broadcasted_iota(jnp.int32, (HEADS, HEADS * WIDTH), 1)
    return jnp.where(col // WIDTH == row, 1.0, 0.0)


def step_sizes(z, bias, rate):
    dt = jax.nn.softplus(z + bias)
    row = lax.broadcasted_iota(jnp.int32, (SPAN, SPAN), 0)
    col = lax.broadcasted_iota(jnp.int32, (SPAN, SPAN), 1)
    upto = jnp.where(row <= col, 1.0, 0.0)
    cums = dot(-rate * dt, upto, precision=HIGH)
    return dt, cums


PIECES = (("x", 0, 48, 80), ("y", 80, 112, 144), ("x", 144, 176, 208), ("y", 208, 240, MSG))
STEPS = sorted(
    ((i, j, k) for i in range(4) for j in range(4) for k in range(2) if i + j + k > 0),
    key=lambda s: -(min(s[0], 4 - s[0]) + min(s[1], 4 - s[1]) + s[2]),
)
NEAR = (0, -1, 1, 2)
EARLY = True
FAR = (2, 1, -1, 0)


def layer_kernel(
    w_hbm,
    wd_ref,
    f_ref,
    x_hbm,
    u_hbm,
    bias_hbm,
    rate_hbm,
    skip_hbm,
    y_hbm,
    dx_hbm,
    gf_hbm,
    grad_ref,
    w_ref,
    bias_ref,
    rate_ref,
    skip_ref,
    rows32,
    f2t,
    gf32,
    gf_ref,
    block,
    x_ref,
    u_ref,
    y_ref,
    dx_ref,
    wt,
    f2,
    kept,
    given,
    taken,
    both,
    r_in,
    msg,
    got,
    out,
    hg,
    ysum,
    esum,
    d_out,
    dp,
    gr,
    r1x,
    r1y,
    acc,
    r2,
    done,
    gf_out,
    gf_in,
    a_send,
    a_recv,
    b_send,
    b_recv,
    c_send,
    c_recv,
    d_send,
    d_recv,
    e_send,
    e_recv,
    local_sem,
    plane_sem,
):
    me = place()
    x, y, zl, zh, core = me
    ring = {"x": x, "y": y}
    span = x * 8 + y * 2 + zl
    partner = {"core": 1 - core}
    beside = {"zl": 1 - zl}
    started = []

    def by(axis, step):
        return {axis: (ring[axis] + step + 4) % 4}

    def span_at(step, sign):
        i, j, k = step
        to = ((x + sign * i + 4) % 4, (y + sign * j + 4) % 4, (zl + k) % 2)
        return to[0] * 8 + to[1] * 2 + to[2], dict(zip(CTX, to))

    def start(copy):
        copy.start()
        started.append(copy)
        return copy

    met = greet(
        [spread_from(*me), beside, by("x", 1), by("x", 3), by("y", 1), by("y", 3), partner]
        + [{"zh": (zh + e) % 4, "zl": 1 - core, "core": zl} for e in range(4)]
    )
    pairs = (
        (w_hbm, w_ref),
        (f_ref, f2.at[zl]),
        (x_hbm, x_ref),
        (u_hbm, u_ref),
        (bias_hbm, bias_ref),
        (rate_hbm, rate_ref),
        (skip_hbm, skip_ref),
    )
    loads = [
        pltpu.make_async_copy(src, dst, local_sem.at[k]) for k, (src, dst) in enumerate(pairs)
    ]
    for copy in loads:
        copy.start()
    loads[0].wait()
    rows32[...] = w_ref[...].astype(F32)
    block[:, :N] = rows32[pl.ds(0, 256, stride=2), :].astype(BF)
    block[:, N:] = rows32[pl.ds(1, 256, stride=2), :].astype(BF)
    met()

    index = {}

    def message(key, block, axis, step):
        k = index.setdefault(key, len(index))
        return remote(block, block, a_send.at[k], a_recv.at[k], by(axis, step))

    def slot(p, a, b, part=0):
        first, lo, mid, hi = PIECES[p]
        lo, hi = ((lo, hi), (lo, mid), (mid, hi))[part]
        i, j = (a, b) if first == "x" else (b, a)
        return wt.at[(x + i + 4) % 4, (y + j + 4) % 4, pl.ds(lo, hi - lo), :]

    def axes(p):
        return ("x", "y") if PIECES[p][0] == "x" else ("y", "x")

    def part_of(step):
        return 1 if step == 1 else 2

    def along(p, d):
        for step in (1, -1):
            start(message(("b", p, d, step), slot(p, d, 0), axes(p)[1], step))

    def along_more(p, d):
        second = axes(p)[1]
        for step in (1, -1):
            message(("b", p, d, step), slot(p, d, -step), second, step).wait_recv()
            start(message(("br", p, d, step), slot(p, d, -step, part_of(step)), second, step))

    def along_end(p, d):
        for step in (1, -1):
            block = slot(p, d, -2 * step, part_of(step))
            message(("br", p, d, step), block, axes(p)[1], step).wait_recv()

    to = spread_to(*me)

    def move(p, here):
        _, lo, _, hi = PIECES[p]
        hi = min(hi, 256)
        dst = wt.at[here[0], here[1], pl.ds(lo, hi - lo)]
        return remote(block.at[pl.ds(lo, hi - lo)], dst, e_send.at[p], e_recv.at[p], to)

    def move_steps(here):
        dst = wt.at[here[0], here[1], pl.ds(256, 16)]
        return remote(wd_ref, dst, e_send.at[5], e_recv.at[5], to)

    every = range(len(PIECES))
    for p in every:
        start(move(p, (to["x"], to["y"])))
    start(move_steps((to["x"], to["y"])))
    swap = remote(f_ref, f2.at[zl], e_send.at[4], e_recv.at[4], beside)
    if EARLY:
        start(swap)
    for p in every:
        move(p, (x, y)).wait_recv()
        if p == every[-1]:
            move_steps((x, y)).wait_recv()
        for step in (1, -1):
            start(message(("a", p, step), slot(p, 0, 0), axes(p)[0], step))
        along(p, 0)
    if not EARLY:
        start(swap)
    lead = [p for p in every if PIECES[p][0] == "x"]
    trail = [p for p in every if PIECES[p][0] == "y"]
    for step in (1, -1):
        for p in every:
            message(("a", p, step), slot(p, -step, 0), axes(p)[0], step).wait_recv()
            start(
                message(("ar", p, step), slot(p, -step, 0, part_of(step)), axes(p)[0], step)
            )
            along(p, -step)
    for p in every:
        along_more(p, 0)
    for p in every:
        for step in (1, -1):
            block = slot(p, -2 * step, 0, part_of(step))
            message(("ar", p, step), block, axes(p)[0], step).wait_recv()
        along(p, 2)
    swaps = []

    def partial_product(i):
        a = (x + NEAR[i] + 4) % 4
        for which, ref in ((1 - core, given), (core, kept)):
            ref[i, 0:256, :] = dot(f2[which], wt[a, :, 0:256, :].reshape(1024, 256))
            ref[i, 256:MSG, :] = sum(
                dot(wt[a, r, 256:MSG, :], f2[which, :, 256 * r : 256 * (r + 1)], NT)
                for r in range(4)
            )
            if ref is given:
                swaps.append(
                    start(remote(given.at[i], taken.at[i], b_send.at[i], b_recv.at[i], partner))
                )

    def pass_on(i):
        swaps[i].wait_recv()
        both[i] = (kept[i] + taken[i]).astype(BF)
        group = (zh - x - NEAR[i] + 8) % 4
        target = {"zh": group, "zl": core, "core": 1 - zl}
        start(remote(both.at[i], r_in.at[i], b_send.at[4 + i], b_recv.at[4 + i], target))

    for p in every:
        along_more(p, -1)
    loads[1].wait()
    remote(f_ref, f2.at[1 - zl], e_send.at[4], e_recv.at[4], beside).wait_recv()
    for p in lead:
        along_end(p, 0)
    partial_product(0)
    for p in every:
        along_more(p, 1)
    for p in every:
        along_more(p, 2)
    pass_on(0)
    for i in (1, 2):
        for p in lead:
            along_end(p, NEAR[i])
        partial_product(i)
        if i == 2:
            pass_on(1)
    for p in lead:
        along_end(p, 2)
    for p in trail:
        for d in NEAR:
            along_end(p, d)
    pl.semaphore_signal(plane_sem, inc=1, device_id=beside, device_id_type=MESH)
    partial_product(3)
    pass_on(2)
    pass_on(3)
    for i in range(4):
        group = (zh - x - NEAR[i] + 8) % 4
        target = {"zh": group, "zl": core, "core": 1 - zl}
        remote(both.at[i], r_in.at[i], b_send.at[4 + i], b_recv.at[4 + i], target).wait_recv()

    proj = sum(r_in[k, 0:256, :].astype(F32) for k in range(4)).astype(BF)
    z = sum(r_in[k, 256:MSG, :].astype(F32) for k in range(4))
    bm, cm = proj[:, :N], proj[:, N:]
    for copy in loads[2:]:
        copy.wait()
    eye = lax.broadcasted_iota(jnp.int32, (HEADS, HEADS), 0)
    eye = eye == lax.broadcasted_iota(jnp.int32, (HEADS, HEADS), 1)

    def column(ref):
        rows = jnp.broadcast_to(ref[...], (HEADS, HEADS))
        return jnp.sum(jnp.where(eye, rows, 0.0), axis=1, keepdims=True)

    bias, rate, gain = column(bias_ref), column(rate_ref), column(skip_ref)
    dt, cums = step_sizes(z, bias, rate)
    last = cums[:, SPAN - 1 : SPAN]
    tail = jnp.exp(last - cums) * dt
    xt = (x_ref[...].astype(F32) * wide(tail)).astype(BF)
    ue = (u_ref[...].astype(F32) * wide(jnp.exp(cums))).astype(BF)
    fresh = dot(xt, bm, TN).astype(BF)
    back = dot(ue, cm, TN).astype(BF)
    decay = jnp.exp(last)
    first = decay.astype(BF).astype(F32)
    second = (decay - first).astype(BF).astype(F32)
    third = decay - first - second
    row16 = lax.broadcasted_iota(jnp.int32, (16, N), 0)
    for s in range(SPANS):
        h = s // 2
        rows = slice(SLICE * s, SLICE * (s + 1))
        msg[s, 0:32, :] = fresh[rows]
        msg[s, 32:64, :] = back[rows]
        pieces = [jnp.broadcast_to(v[h : h + 1, :], (16, N)) for v in (first, second, third)]
        msg[s, 64:80, :] = jnp.where(
            row16 == 0, pieces[0], jnp.where(row16 == 1, pieces[1], pieces[2])
        ).astype(BF)
    pl.semaphore_wait(plane_sem, 1)
    for d, step in enumerate(STEPS):
        p, there = span_at(step, 1)
        start(remote(msg.at[p], got.at[span], c_send.at[0, d], c_recv.at[0, d], there))
    got[span] = msg[span]

    for which in (0, 1):
        f2t[which] = f2[which].T
    scores = dot(cm, bm, NT)
    cols = cums.T
    row = lax.broadcasted_iota(jnp.int32, (SPAN, SPAN), 0)
    col = lax.broadcasted_iota(jnp.int32, (SPAN, SPAN), 1)
    causal = row >= col
    lane = lax.broadcasted_iota(jnp.int32, (SPAN, 2 * WIDTH), 1)
    zero = jnp.zeros((SPAN, 2 * WIDTH), BF)
    dt_cols = dt.T
    dscores = jnp.zeros((SPAN, SPAN), F32)
    for pair in range(HEADS // 2):
        cut = slice(2 * WIDTH * pair, 2 * WIDTH * (pair + 1))
        x2, u2 = x_ref[:, cut], u_ref[:, cut]
        steps = jnp.where(
            lane < WIDTH,
            jnp.broadcast_to(dt_cols[:, 2 * pair : 2 * pair + 1], (SPAN, 2 * WIDTH)),
            jnp.broadcast_to(dt_cols[:, 2 * pair + 1 : 2 * pair + 2], (SPAN, 2 * WIDTH)),
        )
        xd = (x2.astype(F32) * steps).astype(BF)
        y2 = e2 = None
        for k in range(2):
            h = 2 * pair + k
            mine = lane < WIDTH if k == 0 else lane >= WIDTH
            diff = cols[:, h : h + 1] - cums[h : h + 1, :]
            fall = jnp.where(causal, jnp.exp(jnp.minimum(diff, 0.0)), 0.0)
            a = (fall * scores).astype(BF)
            uh = jnp.where(mine, u2, zero)
            yk = dot(a, jnp.where(mine, xd, zero))
            ek = dot(a, uh, TN)
            y2 = yk if y2 is None else y2 + yk
            e2 = ek if e2 is None else e2 + ek
            dscores = dscores + (fall * dt[h : h + 1, :]) * dot(uh, x2, NT)
        ysum[:, cut] = y2
        esum[:, cut] = e2
    ds = dscores.astype(BF)

    for d, step in enumerate(STEPS):
        p, there = span_at(step, -1)
        remote(msg.at[p], got.at[p], c_send.at[0, d], c_recv.at[0, d], there).wait_recv()

    def decay_of(p):
        rows = got[p, 64:80, :].astype(F32)
        return rows[0:1] + rows[1:2] + rows[2:3]

    state = jnp.zeros((SLICE, N), F32)
    for p in range(SPANS):
        out[p, 0:32, :] = state.astype(BF)
        state = decay_of(p) * state + got[p, 0:32, :].astype(F32)
    state = jnp.zeros((SLICE, N), F32)
    for p in reversed(range(SPANS)):
        out[p, 32:64, :] = state.astype(BF)
        state = decay_of(p) * state + got[p, 32:64, :].astype(F32)
    for d, step in enumerate(STEPS):
        p, there = span_at(step, 1)
        start(remote(out.at[p], hg.at[span], c_send.at[1, d], c_recv.at[1, d], there))
    hg[span] = out[span]
    xf, uf = x_ref[...].astype(F32), u_ref[...].astype(F32)
    heads = by_head()
    e_in = esum[...]
    v_in = dot(heads, xf * e_in, NT, HIGH)
    dt_wide = wide(dt)
    grown = wide(jnp.exp(cums))
    left = wide(jnp.exp(last - cums))
    skip = jnp.concatenate(
        [jnp.broadcast_to(gain[h : h + 1, :], (SPAN, WIDTH)) for h in range(HEADS)], axis=1
    )
    from_here = jnp.where(row >= col, 1.0, 0.0)
    before = jnp.where(row < col, 1.0, 0.0)
    for d, step in enumerate(STEPS):
        p, there = span_at(step, -1)
        remote(out.at[p], hg.at[p], c_send.at[1, d], c_recv.at[1, d], there).wait_recv()

    enter = hg[:, 0:32, :].reshape(HEADS * WIDTH, N)
    leave = hg[:, 32:64, :].reshape(HEADS * WIDTH, N)
    d_out[0:256, N:] = (dot(ds, bm) + dot(ue, enter)).astype(BF)
    d_out[0:256, :N] = (dot(ds, cm, TN) + dot(xt, leave)).astype(BF)

    parts = (pl.ds(0, 256), pl.ds(256, 16))

    def share(i, part):
        a = (zh + x + FAR[i] + 4) % 4
        target = {"zh": a, "zl": 1 - core, "core": zl}
        rows, k = parts[part], 8 * part + i
        return remote(d_out.at[rows], dp.at[zl, i, rows], d_send.at[k], d_recv.at[k], target)

    def shared(i, part):
        a = (zh - x - FAR[i] + 8) % 4
        target = {"zh": a, "zl": 1 - core, "core": zl}
        rows, k = parts[part], 8 * part + i
        copy = remote(d_out.at[rows], dp.at[core, i, rows], d_send.at[k], d_recv.at[k], target)
        copy.wait_recv()

    def share_again(i, part, side):
        block, k = dp.at[side, i, parts[part]], 8 * part + 4 + i
        return remote(block, block, d_send.at[k], d_recv.at[k], partner)

    for i in range(4):
        start(share(i, 0))
    y_core = ysum[...] + grown * dot(cm, enter, NT)
    e_out = left * dot(bm, leave, NT)
    q = dot(heads, uf * y_core, NT, HIGH)
    v_out = dot(heads, xf * e_out, NT, HIGH)
    product = dot(heads, leave.astype(F32) * enter.astype(F32), precision=HIGH)
    product = decay * jnp.sum(product, axis=1, keepdims=True)
    dla = dot(q - dt * v_in, from_here, precision=HIGH)
    dla = dla + dot(dt * v_out, before, precision=HIGH) + product
    dz = (v_in + v_out - rate * dla) * jax.nn.sigmoid(z + bias)
    d_out[256:MSG, :] = dz.astype(BF)
    for i in range(4):
        start(share(i, 1))

    y_ref[...] = (y_core + skip * xf).astype(BF)
    dx_ref[...] = (dt_wide * (e_in + e_out) + skip * uf).astype(BF)
    stores = [
        pltpu.make_async_copy(src, dst, local_sem.at[7 + k])
        for k, (src, dst) in enumerate(((y_ref, y_hbm), (dx_ref, dx_hbm)))
    ]
    for copy in stores:
        copy.start()

    def sum_x(i, j):
        block = gr.at[i, (y + FAR[j] + 4) % 4, pl.ds(0, 128), :]
        k = 44 + 4 * i + j
        return remote(block, r1x.at[i, j], e_send.at[k], e_recv.at[k], by("x", FAR[i]))

    def sum_y(i, j):
        block = gr.at[i, (y + FAR[j] + 4) % 4, pl.ds(128, 128), :]
        k = 12 + 4 * i + j
        return remote(block, r1y.at[j, i], e_send.at[k], e_recv.at[k], by("y", FAR[j]))

    def weight_gradient(i):
        share_again(i, 0, 1 - core).wait_recv()
        mine = dot(f2t[0], dp[0, i, 0:256, :]) + dot(f2t[1], dp[1, i, 0:256, :])
        gr[i] = mine.reshape(4, 256, 256).astype(BF)
        if FAR[i] != 0:
            for j in range(4):
                start(sum_x(i, j))
        for j in range(3):
            start(sum_y(i, j))

    def feature_gradient(which, r, blocks):
        slots = [(x + FAR[i] + 4) % 4 for i in blocks]
        dzs = jnp.concatenate([dp[which, i, 256:MSG, :] for i in blocks], axis=0)
        rows = jnp.concatenate([wt[a, r, 256:MSG, :] for a in slots], axis=0)
        total = dot(dzs, rows, TN)
        for i, a in zip(blocks, slots):
            total = total + dot(dp[which, i, 0:256, :], wt[a, r, 0:256, :], NT)
        return total

    for i in range(4):
        shared(i, 0)
        start(share_again(i, 0, core))
        if i > 0:
            weight_gradient(i - 1)
    for i in range(4):
        shared(i, 1)
        start(share_again(i, 1, core))
    weight_gradient(3)
    for i in range(4):
        share_again(i, 1, 1 - core).wait_recv()

    def sum_again(half, j):
        axis = "y" if half == 0 else "x"
        block = acc.at[half, j]
        k = 32 + 4 * half + j
        return remote(block, r2.at[half, j], e_send.at[k], e_recv.at[k], by(axis, FAR[j]))

    backs = []
    for r in range(4):
        gf_out[r] = feature_gradient(1 - zl, r, (0, 1, 2, 3)).astype(BF)
        copy = remote(gf_out.at[r], gf_in.at[r], e_send.at[28 + r], e_recv.at[28 + r], beside)
        backs.append(start(copy))
    for j in range(4):
        total = gr[3, (y + FAR[j] + 4) % 4, 0:128, :].astype(F32)
        for i in range(3):
            sum_x(i, j).wait_recv()
            total = total + r1x[i, j].astype(F32)
        acc[0, j] = total.astype(BF)
        if j < 3:
            start(sum_again(0, j))
    for i in range(4):
        for j in range(3):
            sum_y(i, j).wait_recv()
        total = gr[i, y, 128:256, :].astype(F32)
        for j in range(3):
            total = total + r1y[j, i].astype(F32)
        acc[1, i] = total.astype(BF)
        if i < 3:
            start(sum_again(1, i))
    for r in range(4):
        gf32[r] = feature_gradient(zl, r, (0, 1, 2, 3))
    homes = []
    for half in (0, 1):
        total = acc[half, 3].astype(F32)
        for j in (1, 2, 0):
            sum_again(half, j).wait_recv()
            total = total + r2[half, j].astype(F32)
        done[half] = total.astype(BF)
        copy = remote(
            done.at[half],
            grad_ref.at[half],
            e_send.at[40 + half],
            e_recv.at[40 + half],
            spread_from(*me),
        )
        homes.append(start(copy))
    for r in range(4):
        backs[r].wait_recv()
        gf_ref[r] = (gf32[r] + gf_in[r].astype(F32)).astype(BF)
        part = gf_hbm.at[:, pl.ds(256 * r, 256)]
        stores.append(pltpu.make_async_copy(gf_ref.at[r], part, local_sem.at[9 + r]))
        stores[-1].start()
    for copy in homes:
        copy.wait_recv()
    for copy in started:
        copy.wait_send()
    for copy in stores:
        copy.wait()


def layer(rows, steps, features, x, u, bias, rate, skip):
    dma = pltpu.SemaphoreType.DMA
    return pl.pallas_call(
        layer_kernel,
        name="layer",
        out_shape=(
            jax.ShapeDtypeStruct((SPAN, 1024), BF),
            jax.ShapeDtypeStruct((SPAN, 1024), BF),
            jax.ShapeDtypeStruct((SPAN, 1024), BF),
            jax.ShapeDtypeStruct((2, 128, 256), BF),
        ),
        in_specs=[ANY] * 8,
        out_specs=(ANY, ANY, ANY, VMEM),
        scratch_shapes=[
            pltpu.VMEM((512, N), BF),
            pltpu.VMEM((1, HEADS), F32),
            pltpu.VMEM((1, HEADS), F32),
            pltpu.VMEM((1, HEADS), F32),
            pltpu.VMEM((512, N), F32),
            pltpu.VMEM((2, 1024, SPAN), BF),
            pltpu.VMEM((4, SPAN, 256), F32),
            pltpu.VMEM((4, SPAN, 256), BF),
            pltpu.VMEM((256, 256), BF),
            pltpu.VMEM((SPAN, 1024), BF),
            pltpu.VMEM((SPAN, 1024), BF),
            pltpu.VMEM((SPAN, 1024), BF),
            pltpu.VMEM((SPAN, 1024), BF),
            pltpu.VMEM((4, 4, MSG, 256), BF),
            pltpu.VMEM((2, SPAN, 1024), BF),
            pltpu.VMEM((4, MSG, 256), F32),
            pltpu.VMEM((4, MSG, 256), F32),
            pltpu.VMEM((4, MSG, 256), F32),
            pltpu.VMEM((4, MSG, 256), BF),
            pltpu.VMEM((4, MSG, 256), BF),
            pltpu.VMEM((SPANS, 80, N), BF),
            pltpu.VMEM((SPANS, 80, N), BF),
            pltpu.VMEM((SPANS, 64, N), BF),
            pltpu.VMEM((SPANS, 64, N), BF),
            pltpu.VMEM((SPAN, 1024), F32),
            pltpu.VMEM((SPAN, 1024), F32),
            pltpu.VMEM((MSG, 256), BF),
            pltpu.VMEM((2, 4, MSG, 256), BF),
            pltpu.VMEM((4, 4, 256, 256), BF),
            pltpu.VMEM((3, 4, 128, 256), BF),
            pltpu.VMEM((3, 4, 128, 256), BF),
            pltpu.VMEM((2, 4, 128, 256), BF),
            pltpu.VMEM((2, 3, 128, 256), BF),
            pltpu.VMEM((2, 128, 256), BF),
            pltpu.VMEM((4, SPAN, 256), BF),
            pltpu.VMEM((4, SPAN, 256), BF),
            dma((20 * len(PIECES),)),
            dma((20 * len(PIECES),)),
            dma((8,)),
            dma((8,)),
            dma((2, SPANS)),
            dma((2, SPANS)),
            dma((16,)),
            dma((16,)),
            dma((56,)),
            dma((56,)),
            dma((13,)),
            pltpu.SemaphoreType.REGULAR,
        ],
        compiler_params=pltpu.CompilerParams(collective_id=0, has_side_effects=True),
    )(rows, steps, features, x, u, bias, rate, skip)


def finish_kernel(*refs):
    sources, targets, held, news = refs[:7], refs[7:13], refs[13:20], refs[20:23]
    rows, arrived, stored = refs[23:]
    loads = [
        pltpu.make_async_copy(src, dst, arrived.at[k])
        for k, (src, dst) in enumerate(zip(sources, held))
    ]
    stores = [
        pltpu.make_async_copy(src, dst, stored.at[k])
        for k, (src, dst) in enumerate(zip((*held[4:], *news), targets))
    ]
    for copy in loads:
        copy.start()
    sum_ref, w_ref, fisher_ref, imp_ref = held[:4]
    for k in range(4):
        loads[k].wait()
    for half in (0, 1):
        total = sum_ref[half].astype(F32)
        for k in (0, 1):
            rows[pl.ds(256 * half + k, 128, stride=2), :] = total[:, N * k : N * (k + 1)]
    for k in range(3):
        loads[4 + k].wait()
        stores[k].start()
    grad = rows[...] / TOKENS
    fisher_new = MIX * grad * grad + (1.0 - MIX) * fisher_ref[...]
    delta = -STEP * grad
    news[0][...] = w_ref[...].astype(F32) + delta
    news[1][...] = fisher_new
    news[2][...] = imp_ref[...] + -grad * delta / (0.5 * fisher_new * delta * delta + EPS)
    for copy in stores[3:]:
        copy.start()
    for copy in stores:
        copy.wait()


def finish(y, dx, gf, total, w, fisher, importance):
    wide_out = jax.ShapeDtypeStruct((SPAN, 1024), BF)
    row_out = jax.ShapeDtypeStruct((512, N), F32)
    sources = (total, w, fisher, importance, y, dx, gf)
    return pl.pallas_call(
        finish_kernel,
        name="finish",
        out_shape=(wide_out,) * 3 + (row_out,) * 3,
        in_specs=[ANY] * 7,
        out_specs=(ANY,) * 6,
        scratch_shapes=[pltpu.VMEM(v.shape, v.dtype) for v in sources]
        + [pltpu.VMEM((512, N), F32)] * 4
        + [pltpu.SemaphoreType.DMA((7,)), pltpu.SemaphoreType.DMA((6,))],
    )(*sources)


def local(features, inner, w_bc, w_dt, dt_bias, decay_rate, skip, cotangent, fisher, importance):
    bias, rate, gain = (v.reshape(1, HEADS) for v in (dt_bias, decay_rate, skip))
    rows, fisher_rows, importance_rows = (v.reshape(512, N) for v in (w_bc, fisher, importance))
    outputs, grad_inner, grad_features, total = layer(
        rows, w_dt.T, features, inner, cotangent, bias, rate, gain
    )
    *wides, weight_new, fisher_new, importance_new = finish(
        outputs, grad_inner, grad_features, total, rows, fisher_rows, importance_rows
    )
    news = (v.reshape(w_bc.shape) for v in (weight_new, fisher_new, importance_new))
    return (*wides, *news)


def solution(mesh):
    split = Mesh(mesh.devices.reshape(4, 4, 2, 4, 2), AXES)
    placed = (
        P(CTX, TP),
        P(CTX, TP),
        P(CTX, None, TP),
        P(CTX, TP),
        P(TP),
        P(TP),
        P(TP),
        P(CTX, TP),
        P(CTX, None, TP),
        P(CTX, None, TP),
    )
    return jax.shard_map(
        local,
        mesh=split,
        in_specs=placed,
        out_specs=(
            P(CTX, TP),
            P(CTX, TP),
            P(CTX, TP),
            P(CTX, None, TP),
            P(CTX, None, TP),
            P(CTX, None, TP),
        ),
        check_vma=False,
    )
```

time: 666 us -> 125 us (0.19)
  waiting for transfers between devices: 435 us -> 0 us
  Pallas kernels: 0 us -> 124 us
  local copies, waits for them, and re-layouts: 58.4 us -> 0 us
  matrix products: 55 us -> 0 us
  other arithmetic: 50.7 us -> 0 us
  blocking collectives: 30.8 us -> 0 us
  between operations: 16.6 us -> 0.8 us
  starting transfers between devices: 14.9 us -> 0 us
    all_gather x9 -> x0, waiting for transfers between devices: 364 us -> none  [the longest x1 161 us: in_one_piece(): whole = lax.all_gather(both, axis, axis=dim, tiled=True)]
    pallas_call x0 -> x2, Pallas kernels: none -> 124 us  [the longest x1 121 us: layer(): pl.pallas_call(layer_kernel, name='layer', out_shape=(jax.ShapeDtypeStruc...]
    reduce_scatter x3 -> x0, waiting for transfers between devices: 69.1 us -> none  [summed_rows(): x = lax.psum_scatter(x, axis, scatter_dimension=dim, tiled=True)]
    dot_general x19 -> x0, matrix products: 55 us -> none  [the longest x3 15.4 us: span_pass(): intra = jnp.einsum('ghij,jghp->ighp', weights, xc, precision=HIGH)]
    another operation x23 -> x0, local copies, waits for them, and re-layouts: 17.6 us -> none
    another operation x11 -> x0, other arithmetic: 17.1 us -> none
    all_gather x2 -> x0, blocking collectives: 16.4 us -> none  [prefix_by_axis(): pieces = jax.tree.map(lambda part: lax.all_gather(part, axis), running)]
    unnamed x2 -> x0, blocking collectives: 14.4 us -> none
  transfers between devices with their start and end apart: 14 -> 0, of which waited for: 11 -> 0; matrix products, arithmetic and copies ran while one was open for 18% -> 0% of each run, Pallas kernels for 0% -> 0%
where the time goes in v1:
time: 125 us
  Pallas kernels  124 us (99%)
    pallas_call x1, Pallas kernels, layer(): pl.pallas_call(layer_kernel, name='layer', out_shape=(jax.ShapeDtypeStruc...  121 us
    pallas_call x1, Pallas kernels, finish(): pl.pallas_call(finish_kernel, name='finish', out_shape=(wide_out,) * 3 +...  2.84 us

profile of v1, /device:TPU:110, one launch (start us, length us, event | category | flops | bytes accessed | tf_op | source)
XLA Modules:
  0.0 124.7 jit_solution(2991683478071245896)
XLA Ops:
  0.6 121.0 %layer.1 = (bf16[256,1024]{1,0:T(8,128)(2,1)}, bf16[256,1024]{1,0:T(8,128)(2,1)}, bf16[256,1024]{1,0:T(8,128)(2,1)}, bf16[2,128,256]{2,1,0:T(8,128)(2,1)}) custom-call(bf16[512,128]{1,0:T(8,128)(2,1)} %bitcast.10, bf16[16,256]{1,0:T(8,128)(2,1)} %bitcast.14, bf16[256,1024]{1,0:T(8,128)(2,1)} %f_ref.1, bf16[256,1024]{1,0:T(8,128)(2,1)} %x_hbm.1, ...), custom_call_target="tpu_custom_call" | custom-call | tf_op jit(solution)/shard_map/layer/pallas_call | solution.py:609
  121.6 2.8 %finish.1 = (bf16[256,1024]{1,0:T(8,128)(2,1)}, bf16[256,1024]{1,0:T(8,128)(2,1)}, bf16[256,1024]{1,0:T(8,128)(2,1)}, f32[512,128]{1,0:T(8,128)}, f32[512,128]{1,0:T(8,128)}, /*index=5*/f32[512,128]{1,0:T(8,128)}) custom-call(bf16[2,128,256]{2,1,0:T(8,128)(2,1)} %get-tuple-element.16.refs_0_, bf16[512,128]{1,0:T(8,128)(2,1)} %bitcast.11, ...), custom_call_target="tpu_custom_call" | custom-call | tf_op jit(solution)/shard_map/finish/pallas_call | solution.py:713
